TPU v7x, 32 devices: a whole 2x2x4 slice. The times are simulated.
32 devices in a mesh: dp: 16 (over z, y, core), owner: 2 (over x).
Axes of the slice: x: 2, y: 2, z: 4, core: 2. Of those that a mesh axis runs over, the one named last changes fastest.
Arguments:
- hidden: bfloat16 [2048, 4096], P('dp'), may hold values from -6 to 6
- norm_gain: float32 [4096], replicated, may hold values from 0.3 to 3
- cotangent: bfloat16 [2048, 6144], P('dp'), may hold values from -30 to 30
Outputs:
- update: bfloat16 [6144, 4096], P('dp', 'owner')
All inputs are finite; a program needn't handle non-finite values. Where the computation divides by a largest or mean magnitude, that divisor is 1e-20 or more.
Results may differ from a plain program's by a relative error of at most 0.014.
Values may be sent and summed in bfloat16 or wider, within the bound.
A program may use at most 128 MiB of HBM per device.

v0:
```python
import jax
import jax.numpy as jnp
from jax import lax
from jax.sharding import PartitionSpec as P

TILE = 1024
DAMPING = 0.1


def shards(hidden, norm_gain, cotangent):
    owners = lax.axis_size("owner")
    position = lax.axis_index("owner")
    groups = lax.axis_size("dp")
    tokens_here = hidden.shape[0]
    width = hidden.shape[1]
    out_width = cotangent.shape[1]
    blocks_all = (width + out_width) // TILE
    slots = (blocks_all + owners - 1) // owners
    states = hidden.astype(jnp.float32)
    normed = (
        states * lax.rsqrt(jnp.mean(states * states, axis=1, keepdims=True) + 1e-05) * norm_gain
    ).astype(jnp.bfloat16)
    source = jnp.concatenate([normed, cotangent], axis=1)
    columns = []
    for slot in range(slots):
        block = jnp.minimum(position + slot * owners, blocks_all - 1)
        columns.append(lax.dynamic_slice_in_dim(source, block * TILE, TILE, 1))
    pieces = jnp.stack(columns)
    partial_value = jnp.einsum("stk,stl->skl", pieces, pieces, preferred_element_type=jnp.float32)
    identity = jnp.eye(TILE, dtype=jnp.float32)
    factor = lax.psum(partial_value, "dp")
    matrix = factor / (tokens_here * groups) + DAMPING * identity
    scale = 1.0 / jnp.max(jnp.sum(jnp.abs(matrix), axis=2), axis=1)
    first = 2.0 * scale[:, None, None] * identity - (scale * scale)[:, None, None] * matrix
    first_low = first.astype(jnp.bfloat16)
    matrix_low = matrix.astype(jnp.bfloat16)
    product = jnp.einsum(
        "skl,slm->skm", first_low, matrix_low, preferred_element_type=jnp.float32
    ).astype(jnp.bfloat16)
    inverse = (
        2.0 * first
        - jnp.einsum("skl,slm->skm", product, first_low, preferred_element_type=jnp.float32)
    ).astype(jnp.bfloat16)
    precond = jnp.einsum(
        "stk,skl->stl", pieces, inverse, preferred_element_type=jnp.float32
    ).astype(jnp.bfloat16)
    gathered = lax.all_gather(precond[:, None], "owner", axis=1, tiled=True)
    ordered = gathered.reshape(slots * owners, tokens_here, TILE)[:blocks_all]
    inputs_side = width // TILE
    pre_in = jnp.transpose(ordered[:inputs_side], (1, 0, 2)).reshape(tokens_here, width)
    pre_out = jnp.transpose(ordered[inputs_side:], (1, 0, 2)).reshape(tokens_here, out_width)
    own_rows = width // owners
    mine_in = lax.dynamic_slice_in_dim(pre_in, position * own_rows, own_rows, 1)
    summed = lax.psum_scatter(
        jnp.einsum("tk,tl->kl", pre_out, mine_in, preferred_element_type=jnp.float32).astype(
            jnp.bfloat16
        ),
        "dp",
        scatter_dimension=0,
        tiled=True,
    ).astype(jnp.float32)
    squares = lax.psum(jnp.sum(summed * summed), ("dp", "owner"))
    return (summed * lax.rsqrt(squares / (width * out_width) + 1e-06)).astype(jnp.bfloat16)


def solution(mesh):
    in_specs = (P("dp", None), P(), P("dp", None))
    out_specs = P("dp", "owner")
    return jax.shard_map(shards, mesh=mesh, in_specs=in_specs, out_specs=out_specs, check_vma=False)
```

profile of v0, /device:TPU:0, one launch (start us, length us, event | category | flops | bytes accessed | tf_op | source)
XLA Modules:
  0.0 812.2 jit_solution(15616103901060733694)
XLA Ops:
  6.5 0.0 copy-start
  6.5 0.0 all-reduce.2.cloned.1.call-start
  6.5 1.6 fusion.17
  8.2 1.6 fusion.19
  9.7 0.0 copy-done
  9.8 0.9 bitcast_dynamic-update-slice_fusion.4
  10.6 0.8 bitcast_dynamic-update-slice_fusion.3
  11.5 0.8 bitcast_dynamic-update-slice_fusion.2
  12.3 0.8 bitcast_dynamic-update-slice_fusion.1
  13.1 0.8 bitcast_dynamic-update-slice_fusion
  14.0 11.8 %fusion.36 = f32[5,1024,1024]{2,1,0:T(8,128)} fusion(bf16[5,128,1024]{2,1,0:T(8,128)(2,1)} %bitcast_dynamic-update-slice_fusion), kind=kOutput, calls=%fused_computation.54 | convolution fusion | flops 1342177280 | bytes 22282240 | tf_op jit(solution)/shard_map/stk,stl->skl/dot_general | solution.py:29
  25.8 0.0 all-reduce.2.cloned.1.call-update
  25.8 0.2 all-gather.3.cloned.1.call-start
  26.0 2.4 fusion.14
  28.5 2.5 fusion.13
  30.9 359.7 %all-reduce.2.cloned.1.call-done = f32[5,1024,1024]{2,1,0:T(8,128)} async-done(((f32[5,1024,1024]{2,1,0:T(8,128)}), f32[5,1024,1024]{2,1,0:T(8,128)}) %all-reduce.2.cloned.1.call-update) | async-done | bytes 20971536 | tf_op jit(solution)/shard_map/psum | solution.py:31
  390.7 9.1 %abs_reduce_fusion = f32[5,1024]{1,0:T(8,128)S(1)} fusion(f32[5,1024,1024]{2,1,0:T(8,128)} %all-reduce.2.cloned.1.call-done, f32[1024,1024]{1,0:T(8,128)} %fusion.14), kind=kLoop, calls=%fused_computation.3 | loop fusion | flops 20966400 | bytes 25186304 | tf_op jit(solution)/shard_map/reduce_sum | solution.py:33
  399.8 0.1 reduce_max.9
  399.9 29.7 %fusion.2 = bf16[5,1024,1024]{2,1,0:T(8,128)(2,1)} fusion(f32[5,1024,1024]{2,1,0:T(8,128)} %all-reduce.2.cloned.1.call-done, f32[1024,1024]{1,0:T(8,128)} %fusion.14, f32[5]{0:T(128)S(1)} %mul.110, f32[1024,1024]{1,0:T(8,128)} %fusion.13, f32[5]{0:T(128)S(1)} %get-tuple-element.5), kind=kOutput, calls=%fused_computation.7 | convolution fusion | flops 10784604160 | bytes 39845928 | tf_op jit(solution)/shard_map/skl,slm->skm/dot_general | solution.py:37
  429.7 29.7 %fusion.20 = bf16[5,128,1024]{2,1,0:T(8,128)(2,1)} fusion(bf16[5,128,1024]{2,1,0:T(8,128)(2,1)} %bitcast_dynamic-update-slice_fusion, f32[5,1024,1024]{2,1,0:T(8,128)} %all-reduce.2.cloned.1.call-done, f32[5]{0:T(128)S(1)} %mul.110, f32[1024,1024]{1,0:T(8,128)} %fusion.13, f32[5]{0:T(128)S(1)} %get-tuple-element.5, f32[1024,1024]{1,0:T(8,128)} %fusion.14, ...), kind=kOutput, calls=%fused_computation.35 | convolution fusion | flops 12153651200 | bytes 42467368 | tf_op jit(solution)/shard_map/stk,skl->stl/dot_general | solution.py:44
  459.4 0.0 all-gather.3.cloned.1.call-update
  459.4 0.3 reduce-scatter.2.cloned.1.call-start
  459.7 38.7 %all-gather.3.cloned.1.call-done = bf16[5,256,1024]{2,1,0:T(8,128)(2,1)} async-done(((bf16[5,128,1024]{2,1,0:T(8,128)(2,1)}), bf16[5,256,1024]{2,1,0:T(8,128)(2,1)}) %all-gather.3.cloned.1.call-update) | async-done | bytes 2621456 | tf_op jit(solution)/shard_map/all_gather | solution.py:47
  498.4 0.0 slice-start
  498.4 1.4 slice-done
  499.8 0.9 copy.9
  500.7 1.3 slice.19
  502.0 1.3 copy.10
  503.3 12.7 %convolution_convert_fusion = bf16[6144,2048]{1,0:T(8,128)(2,1)} fusion(bf16[128,6144]{0,1:T(8,128)(2,1)S(1)} %bitcast.23, bf16[128,4096]{0,1:T(8,128)(2,1)} %bitcast.26, s32[]{:T(128)S(6)} %select_n.23), kind=kOutput, calls=%fused_computation | convolution fusion | flops 3233808384 | bytes 27262980 | tf_op jit(solution)/shard_map/tk,tl->kl/dot_general | solution.py:55
  516.0 0.0 reduce-scatter.2.cloned.1.call-update
  516.1 243.7 %reduce-scatter.2.cloned.1.call-done = bf16[384,2048]{1,0:T(8,128)(2,1)} async-done(((bf16[6144,2048]{1,0:T(8,128)(2,1)}), bf16[384,2048]{1,0:T(8,128)(2,1)}) %reduce-scatter.2.cloned.1.call-update) | async-done | bytes 1572880 | tf_op jit(solution)/shard_map/reduce_scatter | solution.py:54
  759.7 2.8 fusion.15
  762.6 39.5 %psum.15 = f32[]{:T(128)} all-reduce(f32[]{:T(128)} %fusion.15), channel_id=1, replica_groups=mesh['dp'=16,'owner'=2] {'dp','owner'}, use_global_device_ids=true, to_apply=%region_6.0 | all-reduce | flops 1 | bytes 8 | tf_op jit(solution)/shard_map/psum | solution.py:62
  802.7 2.9 fusion.16
  (3 shorter events, 0.0 us)
Async XLA Ops:
  6.5 3.2 copy-start
  6.5 384.1 %all-reduce.2.cloned.1.call-start = ((), (), s32[]{:S(2)}) async-start(), calls=%async_computation.1 | async-start | bytes 41943040 | tf_op jit(solution)/shard_map/psum | solution.py:31
  25.8 472.6 %all-gather.3.cloned.1.call-start = ((), (), s32[]{:S(2)}) async-start(), calls=%async_computation.3 | async-start | bytes 3932160 | tf_op jit(solution)/shard_map/all_gather | solution.py:47
  459.4 300.3 %reduce-scatter.2.cloned.1.call-start = ((), (), s32[]{:S(2)}) async-start(), calls=%async_computation.2 | async-start | bytes 26738688 | tf_op jit(solution)/shard_map/reduce_scatter | solution.py:54
  498.4 1.4 slice-start
Sparse Core Ops, SparseCore 0:
  25.9 364.6 all-reduce.1
  459.5 38.8 all-gather.2
  516.2 243.5 reduce-scatter.1
where the time goes:
time: 813 us; the launch traced here: 812 us
  waiting for transfers between devices  642 us (79%)
  matrix products  83.9 us (10%)
  blocking collectives  39.5 us (5%)
  other arithmetic  27.3 us (3%)
  between operations  13.8 us (2%)
    psum x1, waiting for transfers between devices, shards(): factor = lax.psum(partial_value, 'dp')  360 us
    reduce_scatter x1, waiting for transfers between devices, shards(): lax.psum_scatter(jnp.einsum('tk,tl->kl', pre_out, mine_in, preferred_elem...  244 us
    psum x1, blocking collectives, shards(): squares = lax.psum(jnp.sum(summed * summed), ('dp', 'owner'))  39.5 us
    all_gather x1, waiting for transfers between devices, shards(): gathered = lax.all_gather(precond[:, None], 'owner', axis=1, tiled=True)  38.7 us
    dot_general x1, matrix products, shards(): jnp.einsum('skl,slm->skm', first_low, matrix_low, preferred_element_type=...  29.7 us
    dot_general x1, matrix products, shards(): jnp.einsum('stk,skl->stl', pieces, inverse, preferred_element_type=jnp.fl...  29.7 us
  transfers between devices with their start and end apart: 3, of which 3 were waited for; matrix products, arithmetic and copies ran while one was open for 1% of the time, Pallas kernels for 0%

commit v1 on v0

--- a/solution.py
+++ b/solution.py
@@ -28,7 +28,9 @@
     pieces = jnp.stack(columns)
     partial_value = jnp.einsum("stk,stl->skl", pieces, pieces, preferred_element_type=jnp.float32)
     identity = jnp.eye(TILE, dtype=jnp.float32)
-    factor = lax.psum(partial_value, "dp")
+    factor = partial_value
+    for hop in (1, 2, 4, 8):
+        factor = factor + lax.ppermute(factor, "dp", [(dev, dev ^ hop) for dev in range(16)])
     matrix = factor / (tokens_here * groups) + DAMPING * identity
     scale = 1.0 / jnp.max(jnp.sum(jnp.abs(matrix), axis=2), axis=1)
     first = 2.0 * scale[:, None, None] * identity - (scale * scale)[:, None, None] * matrix

time: 813 us -> 2350 us (2.89)
  waiting for transfers between devices: 642 us -> 2110 us
  other arithmetic: 27.3 us -> 76.4 us
    ppermute x0 -> x4, waiting for transfers between devices: none -> 1820 us  [shards(): lax.ppermute(factor, 'dp', [(dev, dev ^ hop) for dev in range(16)])]
    psum x1 -> x0, waiting for transfers between devices: 360 us -> none  [shards(): factor = lax.psum(partial_value, 'dp')]
    add x0 -> x3, other arithmetic: none -> 45.5 us  [shards(): factor + lax.ppermute(factor, 'dp', [(dev, dev ^ hop) for dev in range(16)])]
    dot_general x0 -> x1, matrix products: none -> 25.6 us  [shards(): jnp.einsum('skl,slm->skm', product, first_low, preferred_element_type=jnp...]
  transfers between devices with their start and end apart: 3 -> 6, of which waited for: 3 -> 6; matrix products, arithmetic and copies ran while one was open for 1% -> 0% of each run, Pallas kernels for 0% -> 0%
where the time goes in v1:
time: 2350 us
  waiting for transfers between devices  2110 us (90%)
  matrix products  96.3 us (4%)
  other arithmetic  76.4 us (3%)
  blocking collectives  39.5 us (2%)
    ppermute x4, waiting for transfers between devices, shards(): lax.ppermute(factor, 'dp', [(dev, dev ^ hop) for dev in range(16)])  1820 us
    reduce_scatter x1, waiting for transfers between devices, shards(): lax.psum_scatter(jnp.einsum('tk,tl->kl', pre_out, mine_in, preferred_elem...  244 us
  transfers between devices with their start and end apart: 6, of which 6 were waited for; matrix products, arithmetic and copies ran while one was open for 0% of the time, Pallas kernels for 0%

profile of v1, /device:TPU:0, one launch (start us, length us, event | category | flops | bytes accessed | tf_op | source)
XLA Modules:
  0.0 2351.0 jit_solution(2127298639973354785)
XLA Ops:
  6.5 0.0 copy-start.1
  6.5 0.0 all-gather.3.cloned.1.call-start
  6.5 1.6 fusion.16
  8.2 1.6 fusion.18
  9.7 0.0 copy-done.1
  9.8 0.8 fusion.21
  10.6 0.2 copy.26
  10.7 0.2 copy.22
  10.9 0.2 copy.23
  11.1 0.2 copy.24
  11.3 0.2 copy.25
  11.7 2.9 fusion.28
  14.6 0.6 collective-permute-start
  15.1 30.9 %collective-permute-done = f32[5,1024,1024]{1,2,0:T(8,128)} collective-permute-done((f32[5,1024,1024]{1,2,0:T(8,128)S(1)}, f32[5,1024,1024]{1,2,0:T(8,128)}, u32[]{:S(2)}, u32[]{:S(2)}) %collective-permute-start) | collective-permute-done | bytes 20971552 | tf_op jit(solution)/shard_map/ppermute | solution.py:33
  46.0 17.2 add.79
  63.2 2.9 collective-permute-start.1
  66.1 450.7 %collective-permute-done.1 = f32[5,1024,1024]{1,2,0:T(8,128)} collective-permute-done((f32[5,1024,1024]{1,2,0:T(8,128)}, f32[5,1024,1024]{1,2,0:T(8,128)}, u32[]{:S(2)}, u32[]{:S(2)}) %collective-permute-start.1) | collective-permute-done | bytes 20971552 | tf_op jit(solution)/shard_map/ppermute | solution.py:33
  516.8 14.2 add.80
  531.0 0.0 copy-start
  531.0 1.9 collective-permute-start.2
  532.9 5.1 copy-done
  538.0 444.8 %collective-permute-done.2 = f32[5,1024,1024]{1,2,0:T(8,128)} collective-permute-done((f32[5,1024,1024]{1,2,0:T(8,128)S(1)}, f32[5,1024,1024]{1,2,0:T(8,128)}, u32[]{:S(2)}, u32[]{:S(2)}) %collective-permute-start.2) | collective-permute-done | bytes 20971552 | tf_op jit(solution)/shard_map/ppermute | solution.py:33
  982.7 14.2 add.81
  996.9 2.6 collective-permute-start.3
  999.5 2.5 fusion.12
  1002.0 0.5 fusion.13
  1002.5 895.6 %collective-permute-done.3 = f32[5,1024,1024]{1,2,0:T(8,128)} collective-permute-done((f32[5,1024,1024]{1,2,0:T(8,128)S(1)}, f32[5,1024,1024]{1,2,0:T(8,128)}, u32[]{:S(2)}, u32[]{:S(2)}) %collective-permute-start.3) | collective-permute-done | bytes 20971552 | tf_op jit(solution)/shard_map/ppermute | solution.py:33
  1898.1 18.0 abs_reduce_fusion
  1916.1 0.1 reduce_max.9
  1916.2 38.0 %fusion.47 = bf16[5,1024,1024]{2,1,0:T(8,128)(2,1)} fusion(f32[5,1024,1024]{1,2,0:T(8,128)} %get-tuple-element.8, f32[5]{0:T(128)S(1)} %mul.110, f32[1024,1024]{0,1:T(8,128)} %fusion.12, f32[5]{0:T(128)S(1)} %get-tuple-element.5), kind=kOutput, calls=%fused_computation.7.clone.2 | convolution fusion | flops 10768875520 | bytes 35651624 | tf_op jit(solution)/shard_map/skl,slm->skm/dot_general | solution.py:39
  1954.2 25.6 %fusion.1 = f32[5,1024,1024]{1,2,0:T(8,128)} fusion(f32[5,1024,1024]{1,2,0:T(8,128)} %get-tuple-element.8, f32[5]{0:T(128)S(1)} %mul.110, f32[1024,1024]{0,1:T(8,128)} %fusion.12, f32[5]{0:T(128)S(1)} %get-tuple-element.5, bf16[5,1024,1024]{2,1,0:T(8,128)(2,1)} %fusion.47), kind=kOutput, calls=%fused_computation.6 | convolution fusion | flops 10758389760 | bytes 56623144 | tf_op jit(solution)/shard_map/skl,slm->skm/dot_general | solution.py:44
  1979.8 17.1 fusion.19
  1997.0 0.0 all-gather.3.cloned.1.call-update
  1997.0 0.0 reduce-scatter.2.cloned.1.call-start
  1997.0 39.9 %all-gather.3.cloned.1.call-done = bf16[5,256,1024]{2,1,0:T(8,128)(2,1)} async-done(((bf16[5,128,1024]{2,1,0:T(8,128)(2,1)}), bf16[5,256,1024]{2,1,0:T(8,128)(2,1)}) %all-gather.3.cloned.1.call-update) | async-done | bytes 2621456 | tf_op jit(solution)/shard_map/all_gather | solution.py:49
  2036.9 0.0 slice-start
  2036.9 1.4 slice-done
  2038.3 0.9 copy.34
  2039.2 1.3 slice.19
  2040.5 1.3 copy.35
  2041.8 12.7 convolution_convert_fusion
  2054.5 0.0 reduce-scatter.2.cloned.1.call-update
  2054.6 243.7 %reduce-scatter.2.cloned.1.call-done = bf16[384,2048]{1,0:T(8,128)(2,1)} async-done(((bf16[6144,2048]{1,0:T(8,128)(2,1)}), bf16[384,2048]{1,0:T(8,128)(2,1)}) %reduce-scatter.2.cloned.1.call-update) | async-done | bytes 1572880 | tf_op jit(solution)/shard_map/reduce_scatter | solution.py:56
  2298.3 2.8 fusion.14
  2301.1 39.5 %psum.7 = f32[]{:T(128)} all-reduce(f32[]{:T(128)} %fusion.14), channel_id=1, replica_groups=mesh['dp'=16,'owner'=2] {'dp','owner'}, use_global_device_ids=true, to_apply=%region_5.0 | all-reduce | flops 1 | bytes 8 | tf_op jit(solution)/shard_map/psum | solution.py:64
  2341.3 2.9 fusion.15
  (8 shorter events, 0.2 us)
Async XLA Ops:
  6.5 3.2 copy-start.1
  6.5 2030.4 %all-gather.3.cloned.1.call-start = ((), (), s32[]{:S(2)}) async-start(), calls=%async_computation.2 | async-start | bytes 3932160 | tf_op jit(solution)/shard_map/all_gather | solution.py:49
  14.6 31.5 %collective-permute-start = (f32[5,1024,1024]{1,2,0:T(8,128)S(1)}, f32[5,1024,1024]{1,2,0:T(8,128)}, u32[]{:S(2)}, u32[]{:S(2)}) collective-permute-start(f32[5,1024,1024]{1,2,0:T(8,128)S(1)} %fusion.28), channel_id=1, source_target_pairs={{0,2},{2,0},{4,6},{6,4},{8,10},{10,8},{12,14},{14,12},{16,18},{18,... | collective-permute-start | bytes 62914568 | tf_op jit(solution)/shard_map/ppermute | solution.py:33
  63.2 453.6 %collective-permute-start.1 = (f32[5,1024,1024]{1,2,0:T(8,128)}, f32[5,1024,1024]{1,2,0:T(8,128)}, u32[]{:S(2)}, u32[]{:S(2)}) collective-permute-start(f32[5,1024,1024]{1,2,0:T(8,128)} %add.79), channel_id=1, source_target_pairs={{0,4},{2,6},{4,0},{6,2},{8,12},{10,14},{12,8},{14,10},{16,20},{18,... | collective-permute-start | bytes 62914568 | tf_op jit(solution)/shard_map/ppermute | solution.py:33
  531.0 7.0 copy-start
  531.0 451.7 %collective-permute-start.2 = (f32[5,1024,1024]{1,2,0:T(8,128)S(1)}, f32[5,1024,1024]{1,2,0:T(8,128)}, u32[]{:S(2)}, u32[]{:S(2)}) collective-permute-start(f32[5,1024,1024]{1,2,0:T(8,128)S(1)} %add.80), channel_id=1, source_target_pairs={{0,8},{2,10},{4,12},{6,14},{8,0},{10,2},{12,4},{14,6},{16,24},{18,... | collective-permute-start | bytes 62914568 | tf_op jit(solution)/shard_map/ppermute | solution.py:33
  996.9 901.2 %collective-permute-start.3 = (f32[5,1024,1024]{1,2,0:T(8,128)S(1)}, f32[5,1024,1024]{1,2,0:T(8,128)}, u32[]{:S(2)}, u32[]{:S(2)}) collective-permute-start(f32[5,1024,1024]{1,2,0:T(8,128)S(1)} %add.81), channel_id=1, source_target_pairs={{0,16},{2,18},{4,20},{6,22},{8,24},{10,26},{12,28},{14,30},{16,0},... | collective-permute-start | bytes 62914568 | tf_op jit(solution)/shard_map/ppermute | solution.py:33
  1997.0 301.3 %reduce-scatter.2.cloned.1.call-start = ((), (), s32[]{:S(2)}) async-start(), calls=%async_computation.1 | async-start | bytes 26738688 | tf_op jit(solution)/shard_map/reduce_scatter | solution.py:56
  2036.9 1.4 slice-start
Sparse Core Ops, SparseCore 0:
  1997.1 39.7 all-gather.2
  2054.7 243.5 reduce-scatter.1
